TPU v7x, 32 devices: a whole 2x2x4 slice. The times are simulated.
32 devices in a mesh: sky: 2 (over x), seg: 16 (over z, y, core).
Axes of the slice: x: 2, y: 2, z: 4, core: 2. Of those that a mesh axis runs over, the one named last changes fastest.
Arguments:
- strain_series: bfloat16 [32, 2, 65536], P(('sky', 'seg')), parts along dimension 0, may hold values from -6 to 6
- antenna: float32 [32, 2, 65536], P(('sky', 'seg')), parts along dimension 0, may hold values from -160 to 160, as said below
- drift: int32 [32, 6], P(('sky', 'seg')), parts along dimension 0, may hold values from -2 to 2
- tracks: int32 [64, 16], replicated, may hold values from 0 to 5
Outputs:
- track_stat: float32 [128, 65536], P('sky', 'seg'), parts along dimension 0
There are 2 independent parts, one for each index of `sky`. A program takes and returns all parts, laid end to end along the dimension named above; an argument that names none is the same for every part. Nothing has to cross between parts.
Inputs may be any that keep to these rules, and one draw needn't show every extreme that they name: `antenna`: row 0 holds the a weights, row 1 the b weights of each segment.
All inputs are finite; a program needn't handle non-finite values.
Results may differ from a plain program's by a relative error of at most 0.0015.
Values sent between devices are 32-bit elements; how exact they have to be, the bound alone decides.
A program may use at most 192 MiB of HBM per device.

v0:
```python
import math

import jax
import jax.numpy as jnp
from jax import lax
from jax.sharding import PartitionSpec as P

DFT_ROWS = 256
BLK = 128
DMAX = 2
KCOH = 6


chirp_step = 3.0
tiny_eps = 1e-06


def section_tables(points, first_rows):
    second_rows = points // first_rows
    outer_index = jnp.arange(first_rows, dtype=jnp.int32)
    inner_index = jnp.arange(second_rows, dtype=jnp.int32)
    first_angle = (
        2.0
        * math.pi
        / first_rows
        * (outer_index[:, None] * outer_index[None, :] % first_rows).astype(jnp.float32)
    )
    cos_one, sin_one = (jnp.cos(first_angle), jnp.sin(first_angle))
    left_table = jnp.stack([jnp.stack([cos_one, sin_one]), jnp.stack([-sin_one, cos_one])]).astype(
        jnp.bfloat16
    )
    second_angle = (
        2.0
        * math.pi
        / second_rows
        * (inner_index[:, None] * inner_index[None, :] % second_rows).astype(jnp.float32)
    )
    cos_two, sin_two = (jnp.cos(second_angle), jnp.sin(second_angle))
    right_table = jnp.stack([jnp.stack([cos_two, -sin_two]), jnp.stack([sin_two, cos_two])]).astype(
        jnp.bfloat16
    )
    twist_angle = (
        2.0
        * math.pi
        / points
        * (outer_index[:, None] * inner_index[None, :] % points).astype(jnp.float32)
    )
    return (left_table, right_table, jnp.cos(twist_angle), jnp.sin(twist_angle))


def coherent_stat(series, weights):
    seg_rows = series.shape[0]
    points = series.shape[2]
    left_table, right_table, twist_cos, twist_sin = section_tables(points, DFT_ROWS)
    second_rows = points // DFT_ROWS
    position = jnp.arange(points, dtype=jnp.float32) / points
    chirp_rate = (jnp.arange(KCOH, dtype=jnp.float32) - (KCOH - 1) / 2.0) * chirp_step
    phases = 2.0 * math.pi * chirp_rate[:, None] * (position * position)[None, :]
    phase_cos, phase_sin = (jnp.cos(phases), jnp.sin(phases))
    series_real = series[:, 0].astype(jnp.float32)[:, None, :]
    series_imag = series[:, 1].astype(jnp.float32)[:, None, :]
    demod_real = series_real * phase_cos + series_imag * phase_sin
    demod_imag = series_imag * phase_cos - series_real * phase_sin
    weight_a = weights[:, 0][:, None, :]
    weight_b = weights[:, 1][:, None, :]
    with_a = jnp.stack([weight_a * demod_real, weight_a * demod_imag], 2)
    with_b = jnp.stack([weight_b * demod_real, weight_b * demod_imag], 2)
    weighted = jnp.stack([with_a, with_b], 2).astype(jnp.bfloat16)
    weighted = weighted.reshape(seg_rows * KCOH * 2, 2, DFT_ROWS, second_rows)
    section_one = jnp.einsum(
        "oikn,binm->bokm", left_table, weighted, preferred_element_type=jnp.float32
    )
    one_real, one_imag = (section_one[:, 0], section_one[:, 1])
    twisted_real = one_real * twist_cos + one_imag * twist_sin
    twisted_imag = one_imag * twist_cos - one_real * twist_sin
    middle = jnp.stack([twisted_real, twisted_imag], 1).astype(jnp.bfloat16)
    spectra = jnp.einsum("bikm,ioml->bolk", middle, right_table, preferred_element_type=jnp.float32)
    spectra = spectra.reshape(seg_rows, KCOH, 2, 2, points)
    a_real, a_imag = (spectra[:, :, 0, 0], spectra[:, :, 0, 1])
    b_real, b_imag = (spectra[:, :, 1, 0], spectra[:, :, 1, 1])
    weight_aa = jnp.mean(weights[:, 0] * weights[:, 0], axis=-1) + tiny_eps
    weight_bb = jnp.mean(weights[:, 1] * weights[:, 1], axis=-1) + tiny_eps
    weight_ab = jnp.mean(weights[:, 0] * weights[:, 1], axis=-1)
    determinant = jnp.maximum(
        weight_aa * weight_bb - weight_ab * weight_ab, 0.1 * weight_aa * weight_bb
    )
    energy = (
        weight_bb[:, None, None] * (a_real * a_real + a_imag * a_imag)
        + weight_aa[:, None, None] * (b_real * b_real + b_imag * b_imag)
        - 2.0 * weight_ab[:, None, None] * (a_real * b_real + a_imag * b_imag)
    )
    return energy / (points * determinant[:, None, None])


def drift_blocks(padded, offsets, extent, amount):
    summed = jnp.zeros(padded.shape[:-2] + (amount, padded.shape[-1]), padded.dtype)
    for offset in range(-extent, extent + 1):
        window = padded[..., extent - offset : extent - offset + amount, :]
        summed = summed + jnp.where((offsets == offset)[..., None, None], window, 0.0)
    return summed


def shift_local(stats, drift):
    seg_rows = stats.shape[0]
    points = stats.shape[2]
    blocks = stats.reshape(seg_rows, KCOH, points // BLK, BLK)
    padded = jnp.pad(blocks, ((0, 0), (0, 0), (DMAX, DMAX), (0, 0)))
    return drift_blocks(padded, drift, DMAX, points // BLK).reshape(seg_rows, KCOH, points)


def track_combine(tracks, moved):
    levels = jnp.arange(KCOH, dtype=jnp.int32)
    pick = (tracks[:, :, None] == levels[None, None, :]).astype(jnp.float32)
    return jnp.einsum("jsk,skf->jf", pick, moved, precision=lax.Precision.HIGHEST)


def local(strain_series, antenna, drift, tracks):
    stats = coherent_stat(strain_series, antenna)
    seg_rows = stats.shape[0]
    segments = tracks.shape[1]
    shifted = shift_local(stats, drift)
    start = lax.axis_index("seg") * seg_rows
    mine = lax.dynamic_slice_in_dim(tracks, start, seg_rows, 1)
    partial_sum = track_combine(mine, shifted)
    result = lax.psum_scatter(partial_sum, "seg", scatter_dimension=1, tiled=True) / segments
    return result


def solution(mesh):
    return jax.shard_map(
        local,
        mesh=mesh,
        in_specs=(
            P(("sky", "seg"), None, None),
            P(("sky", "seg"), None, None),
            P(("sky", "seg"), None),
            P(),
        ),
        out_specs=P("sky", "seg"),
        check_vma=False,
    )
```

profile of v0, /device:TPU:0, one launch (start us, length us, event | category | flops | bytes accessed | tf_op | source)
XLA Modules:
  0.0 317.6 jit_solution(17125670687759056328)
XLA Ops:
  6.5 0.0 copy-start
  6.5 0.0 copy-start.2
  6.5 0.0 reduce-scatter.2.cloned.1.call-start
  6.6 1.0 fusion.35
  7.5 0.1 multiply_multiply_fusion
  7.6 1.8 negate_convert_fusion
  9.4 1.7 fusion.32
  11.1 1.2 compare_bitcast_fusion.4
  12.4 1.5 slice_convert_fusion
  13.8 0.0 copy-done.2
  13.8 1.9 multiply_reduce_fusion
  19.1 49.6 %multiply_convert_fusion.3 = (bf16[1,6,1,65536]{3,2,1,0:T(2,128)(2,1)S(1)}, bf16[1,6,1,65536]{3,2,1,0:T(2,128)(2,1)S(1)}, bf16[1,6,1,65536]{3,2,1,0:T(2,128)(2,1)S(1)}, bf16[1,6,1,65536]{3,2,1,0:T(2,128)(2,1)S(1)}) fusion(f32[65536]{0:T(1024)S(1)} %bitcast.78, f32[65536]{0:T(1024)S(1)} %bitcast.80, f32[65536]{0:T(1024)S(1)} %multiply_multiply_fusion, ...), kind=kLoop, calls=%fused_computation.26 | loop fusion | flops 5898240 | bytes 4456472 | tf_op jit(solution)/shard_map/convert.18
  68.8 6.7 %maximum_bitcast_fusion.4 = (bf16[1,6,1,2,65536]{4,3,2,1,0:T(2,128)(2,1)S(1)}, bf16[1,6,1,2,65536]{4,3,2,1,0:T(2,128)(2,1)S(1)}) fusion(bf16[1,6,1,65536]{3,2,1,0:T(2,128)(2,1)S(1)} %get-tuple-element.11, bf16[1,6,1,65536]{3,2,1,0:T(2,128)(2,1)S(1)} %get-tuple-element.10, bf16[1,6,1,65536]{3,2,1,0:T(2,128)(2,1)S(1)} %get-tuple-element.14, ...), kind=kLoop, calls=%fused_computation.16 | loop fusion | flops 6291456 | bytes 6291456 | tf_op jit(solution)/shard_map/stack | solution.py:68
  75.5 4.5 %pad_maximum_fusion = bf16[1,6,2,2,65536]{4,3,2,1,0:T(2,128)(2,1)S(1)} fusion(bf16[1,6,1,2,65536]{4,3,2,1,0:T(2,128)(2,1)S(1)} %get-tuple-element.32, bf16[1,6,1,2,65536]{4,3,2,1,0:T(2,128)(2,1)S(1)} %get-tuple-element.31), kind=kLoop, calls=%fused_computation | loop fusion | flops 1572864 | bytes 6291456 | tf_op jit(solution)/shard_map/stack | solution.py:68
  80.0 5.4 %convert_element_type.71 = bf16[12,2,256,256]{3,2,1,0:T(8,128)(2,1)} reshape(bf16[1,6,2,2,65536]{4,3,2,1,0:T(2,128)(2,1)S(1)} %pad_maximum_fusion) | data formatting | bytes 6291456 | tf_op jit(solution)/shard_map/convert_element_type | solution.py:68
  85.5 1.2 fusion.18
  86.7 0.0 copy-start.1
  86.7 3.8 %fusion.5 = f32[12,2,256,256]{2,3,1,0:T(8,128)S(1)} fusion(bf16[12,2,256,256]{3,2,1,0:T(8,128)(2,1)} %convert_element_type.71, bf16[1,2,256,256]{3,2,1,0:T(8,128)(2,1)S(1)} %get-tuple-element.19, bf16[1,2,256,256]{3,2,1,0:T(8,128)(2,1)S(1)} %get-tuple-element.24), kind=kOutput, calls=%fused_computation.9 | convolution fusion | flops 1611661312 | bytes 9961472 | tf_op jit(solution)/shard_map/oikn,binm->bokm/dot_general | solution.py:70
  90.5 0.0 copy-done.1
  90.5 0.9 add_convert_fusion
  91.4 4.5 %fusion.8 = f32[12,2,256,256]{3,2,0,1:T(8,128)} fusion(bf16[12,1,256,256]{2,3,1,0:T(8,128)(2,1)S(1)} %get-tuple-element.9, bf16[12,1,256,256]{2,3,1,0:T(8,128)(2,1)S(1)} %get-tuple-element.8, bf16[1,2,256,256]{3,2,1,0:T(8,128)(2,1)S(1)} %get-tuple-element.25, bf16[1,2,256,256]{3,2,1,0:T(8,128)(2,1)S(1)} %get-tuple-element.18), kind=kOutput, calls=%fused_computation.10 | convolution fusion | flops 1617166336 | bytes 9961472 | tf_op jit(solution)/shard_map/bikm,ioml->bolk/dot_general | solution.py:77
  95.8 10.9 %reshape.1140 = f32[1,6,2,2,65536]{4,2,1,3,0:T(2,128)} reshape(f32[12,2,256,256]{3,2,0,1:T(8,128)} %fusion.8) | data formatting | bytes 12582912 | tf_op jit(solution)/shard_map/reshape | solution.py:78
  106.8 0.0 copy-done
  106.8 0.0 copy-start.3
  106.8 0.0 copy-start.4
  106.8 0.0 copy-start.5
  106.8 9.9 %subtract_divide_fusion = f32[1,6,1,1,65536]{4,2,1,3,0:T(1,128)S(1)} fusion(f32[1,6,2,2,65536]{4,2,1,3,0:T(2,128)} %reshape.1140, f32[]{:T(128)} %bitcast.28, f32[]{:T(128)S(6)} %mul.738, f32[]{:T(128)} %add.192, f32[]{:T(128)} %add.186), kind=kLoop, calls=%fused_computation.18 | loop fusion | flops 5898240 | bytes 7864336 | tf_op jit(solution)/shard_map/div | solution.py:92
  116.8 0.0 copy-done.3
  116.8 0.0 copy-done.4
  116.8 0.0 copy-done.5
  116.8 1.3 add_bitcast_fusion
  118.1 10.2 %fusion.9 = f32[64,65536]{1,0:T(8,128)} fusion(f32[1,6,512,128]{3,2,1,0:T(8,128)S(1)} %add_bitcast_fusion, s32[64]{0:T(128)S(1)} %dynamic-slice_bitcast_fusion), kind=kOutput, calls=%fused_computation.11 | convolution fusion | flops 301990272 | bytes 18350336 | tf_op jit(solution)/shard_map/jsk,skf->jf/dot_general | solution.py:114
  128.3 0.0 reduce-scatter.2.cloned.1.call-update
  128.3 180.1 %reduce-scatter.2.cloned.1.call-done = f32[64,4096]{1,0:T(8,128)} async-done(((f32[64,65536]{1,0:T(8,128)}), f32[64,4096]{1,0:T(8,128)}) %reduce-scatter.2.cloned.1.call-update) | async-done | bytes 1048592 | tf_op jit(solution)/shard_map/reduce_scatter | solution.py:125
  308.4 2.3 broadcast_multiply_fusion
  (2 shorter events, 0.0 us)
Async XLA Ops:
  6.5 100.2 %copy-start = (s32[64,16]{0,1:T(8,128)S(1)}, s32[64,16]{0,1:T(8,128)}, u32[]{:S(2)}) copy-start(s32[64,16]{0,1:T(8,128)} %param.7) | copy-start | bytes 12292
  6.5 7.3 %copy-start.2 = (f32[1,2,65536]{2,1,0:T(2,128)S(1)}, f32[1,2,65536]{2,1,0:T(2,128)}, u32[]{:S(2)}) copy-start(f32[1,2,65536]{2,1,0:T(2,128)} %param.5) | copy-start | bytes 1572868
  6.5 301.9 %reduce-scatter.2.cloned.1.call-start = ((), (), s32[]{:S(2)}) async-start(), calls=%async_computation.1 | async-start | bytes 17825792 | tf_op jit(solution)/shard_map/reduce_scatter | solution.py:125
  86.7 3.8 %copy-start.1 = (f32[256,256]{0,1:T(8,128)S(1)}, f32[256,256]{0,1:T(8,128)}, u32[]{:S(2)}) copy-start(f32[256,256]{0,1:T(8,128)} %get-tuple-element.36) | copy-start | bytes 786436
  106.8 10.0 %copy-start.3 = (pred[6]{0:T(512)(128)(4,1)S(1)}, pred[6]{0:T(512)(128)(4,1)}, u32[]{:S(2)}) copy-start(pred[6]{0:T(512)(128)(4,1)} %get-tuple-element.28) | copy-start | bytes 22
  106.8 10.0 %copy-start.4 = (pred[6]{0:T(512)(128)(4,1)S(1)}, pred[6]{0:T(512)(128)(4,1)}, u32[]{:S(2)}) copy-start(pred[6]{0:T(512)(128)(4,1)} %get-tuple-element.29) | copy-start | bytes 22
  106.8 10.0 %copy-start.5 = (pred[6]{0:T(512)(128)(4,1)S(1)}, pred[6]{0:T(512)(128)(4,1)}, u32[]{:S(2)}) copy-start(pred[6]{0:T(512)(128)(4,1)} %get-tuple-element.30) | copy-start | bytes 22
Sparse Core Ops, SparseCore 0:
  128.5 179.9 reduce-scatter.1
where the time goes:
time: 318 us
  waiting for transfers between devices  180 us (57%)
  other arithmetic  85.7 us (27%)
  matrix products  18.4 us (6%)
  between operations  16.9 us (5%)
  local copies, waits for them, and re-layouts  16.4 us (5%)
    reduce_scatter x1, waiting for transfers between devices, local(): lax.psum_scatter(partial_sum, 'seg', scatter_dimension=1, tiled=True)  180 us
    another operation x4, other arithmetic  53.3 us
    another operation x2, other arithmetic, coherent_stat(): weighted = jnp.stack([with_a, with_b], 2).astype(jnp.bfloat16)  11.2 us
    reshape x1, local copies, waits for them, and re-layouts, coherent_stat(): spectra = spectra.reshape(seg_rows, KCOH, 2, 2, points)  10.9 us
    dot_general x1, matrix products, track_combine(): jnp.einsum('jsk,skf->jf', pick, moved, precision=lax.Precision.HIGHEST)  10.2 us
    div x1, other arithmetic, coherent_stat(): return energy / (points * determinant[:, None, None])  9.93 us
  transfers between devices with their start and end apart: 1, of which 1 were waited for; matrix products, arithmetic and copies ran while one was open for 0% of the time, Pallas kernels for 0%

commit v1 on v0

v1 whole, which is shorter than its diff:
```python
import functools
import math

import jax
import jax.numpy as jnp
import numpy as np
from jax import lax
from jax.experimental import pallas as pl
from jax.experimental.pallas import tpu as pltpu
from jax.sharding import PartitionSpec as P

DFT_ROWS = 256
BLK = 128
DMAX = 2
KCOH = 6
PAD = 8

chirp_step = 3.0
tiny_eps = 1e-06


def dft_table(rows):
    index = np.arange(rows, dtype=np.int64)
    angle = np.float32(2.0 * math.pi / rows) * (index[:, None] * index[None, :] % rows).astype(np.float32)
    cos, sin = np.cos(angle), np.sin(angle)
    return np.block([[cos, sin], [-sin, cos]]).astype(jnp.bfloat16)


def twist_table(points, first_rows):
    second_rows = points // first_rows
    outer = np.arange(first_rows, dtype=np.int64)
    inner = np.arange(second_rows, dtype=np.int64)
    angle = np.float32(2.0 * math.pi / points) * (outer[:, None] * inner[None, :] % points).astype(np.float32)
    return np.stack([np.cos(angle), np.sin(angle)]).astype(np.float32)


def chirp_table(points, first_rows):
    position = np.arange(points, dtype=np.float32) / np.float32(points)
    rate = (np.arange(KCOH // 2, KCOH, dtype=np.float32) - np.float32((KCOH - 1) / 2.0)) * np.float32(chirp_step)
    phases = (np.float32(2.0 * math.pi) * rate)[:, None] * (position * position)[None, :]
    both = np.stack([np.cos(phases), np.sin(phases)], 1).astype(np.float32)
    return both.reshape(KCOH // 2, 2, first_rows, points // first_rows)


def kernel(
    count, drift_ref, series_ref, antenna_ref, chirp_ref, twist_ref, first_ref, second_ref, pick_ref, out_ref,
    weighted, spread, middle, padded, send, recv, send_sem, recv_sem,
):
    _, first_rows, second_rows = series_ref.shape
    rows = second_rows // count
    points = first_rows * second_rows
    halves = first_rows // BLK
    sky = lax.axis_index("sky")
    me = lax.axis_index("seg")

    barrier = pltpu.get_barrier_semaphore()

    def greet(step, carry):
        pl.semaphore_signal(
            barrier, inc=1, device_id=(sky, lax.rem(me + step, count)), device_id_type=pl.DeviceIdType.MESH
        )
        return carry

    lax.fori_loop(1, count, greet, 0)

    weight_a, weight_b = antenna_ref[0], antenna_ref[1]
    total = lambda value: jnp.sum(jnp.sum(value, axis=0, keepdims=True), axis=1, keepdims=True)
    aa = total(weight_a * weight_a) / points + tiny_eps
    bb = total(weight_b * weight_b) / points + tiny_eps
    ab = total(weight_a * weight_b) / points
    scale = 1.0 / (points * jnp.maximum(aa * bb - ab * ab, 0.1 * aa * bb))
    coef_a, coef_b, coef_ab = bb * scale, aa * scale, 2.0 * ab * scale

    for half in range(halves):
        padded[half, :PAD] = jnp.zeros((PAD, BLK), jnp.float32)
        padded[half, PAD + second_rows :] = jnp.zeros((PAD, BLK), jnp.float32)

    pl.semaphore_wait(barrier, count - 1)

    def one_rate(k, carry):
        upper = k >= KCOH // 2
        level = jnp.where(upper, k - KCOH // 2, KCOH // 2 - 1 - k)
        sign = jnp.where(upper, 1.0, -1.0)
        chirp_cos = chirp_ref[level, 0]
        chirp_sin = chirp_ref[level, 1] * sign
        real, imag = series_ref[0].astype(jnp.float32), series_ref[1].astype(jnp.float32)
        demod_real = real * chirp_cos + imag * chirp_sin
        demod_imag = imag * chirp_cos - real * chirp_sin
        for which in range(2):
            weight = antenna_ref[which]
            columns = slice(which * second_rows, (which + 1) * second_rows)
            weighted[:first_rows, columns] = (weight * demod_real).astype(jnp.bfloat16)
            weighted[first_rows:, columns] = (weight * demod_imag).astype(jnp.bfloat16)
        spread[...] = jnp.dot(first_ref[...], weighted[...], preferred_element_type=jnp.float32)
        twist_cos, twist_sin = twist_ref[0], twist_ref[1]
        for which in range(2):
            columns = slice(which * second_rows, (which + 1) * second_rows)
            one_real, one_imag = spread[:first_rows, columns], spread[first_rows:, columns]
            lines = slice(which * first_rows, (which + 1) * first_rows)
            middle[lines, :second_rows] = (one_real * twist_cos + one_imag * twist_sin).astype(jnp.bfloat16)
            middle[lines, second_rows:] = (one_imag * twist_cos - one_real * twist_sin).astype(jnp.bfloat16)
        spread[...] = lax.dot_general(
            second_ref[...], middle[...], (((1,), (1,)), ((), ())), preferred_element_type=jnp.float32
        )
        for half in range(halves):
            at_a = slice(half * BLK, (half + 1) * BLK)
            at_b = slice(first_rows + half * BLK, first_rows + (half + 1) * BLK)
            a_real, a_imag = spread[:second_rows, at_a], spread[second_rows:, at_a]
            b_real, b_imag = spread[:second_rows, at_b], spread[second_rows:, at_b]
            padded[half, PAD : PAD + second_rows] = (
                coef_a * (a_real * a_real + a_imag * a_imag)
                + coef_b * (b_real * b_real + b_imag * b_imag)
                - coef_ab * (a_real * b_real + a_imag * b_imag)
            )
        shift = drift_ref[0, k]

        def place(peer, inner):
            for half in range(halves):
                block = half - shift + halves * PAD
                source = lax.rem(block, halves)
                start = lax.div(block, halves) + rows * peer
                send[k, peer, :, half * BLK : (half + 1) * BLK] = padded[source, pl.ds(start, rows), :]
            return inner

        lax.fori_loop(0, count, place, 0)

        def ship(step, inner):
            peer = lax.rem(me + step, count)
            pltpu.make_async_remote_copy(
                src_ref=send.at[k, peer],
                dst_ref=recv.at[k, me],
                send_sem=send_sem.at[k],
                recv_sem=recv_sem.at[k],
                device_id=(sky, peer),
                device_id_type=pl.DeviceIdType.MESH,
            ).start()
            return inner

        lax.fori_loop(count // 2, count, ship, 0)
        lax.fori_loop(1, count // 2, ship, 0)
        pltpu.make_async_copy(send.at[k, me], recv.at[k, me], recv_sem.at[k]).start()
        return carry

    lax.fori_loop(0, KCOH, one_rate, 0)

    for k in range(KCOH):
        pltpu.make_async_copy(recv.at[k], recv.at[k], recv_sem.at[k]).wait()

    pick = pick_ref[...]
    for row in range(rows):
        value = recv[:, :, row, :].reshape(KCOH * count, first_rows)
        high = value.astype(jnp.bfloat16)
        low = (value - high.astype(jnp.float32)).astype(jnp.bfloat16)
        out_ref[:, row * first_rows : (row + 1) * first_rows] = jnp.dot(
            pick, jnp.concatenate([high, low], 0), preferred_element_type=jnp.float32
        )

    for k in range(KCOH):
        part = send.at[k, pl.ds(0, count - 1)]
        pltpu.make_async_copy(part, part, send_sem.at[k]).wait()


def local(count, strain_series, antenna, drift, tracks):
    points = strain_series.shape[2]
    first_rows, second_rows = DFT_ROWS, points // DFT_ROWS
    segments = tracks.shape[1]
    rows = second_rows // count
    levels = jnp.arange(KCOH, dtype=jnp.int32)
    pick = (tracks[:, None, :] == levels[None, :, None]).astype(jnp.bfloat16)
    pick = pick.reshape(tracks.shape[0], KCOH * segments)
    vmem = pl.BlockSpec(memory_space=pltpu.VMEM)
    summed = pl.pallas_call(
        functools.partial(kernel, count),
        out_shape=jax.ShapeDtypeStruct((tracks.shape[0], points // count), jnp.float32),
        in_specs=[pl.BlockSpec(memory_space=pltpu.SMEM)] + [vmem] * 7,
        out_specs=vmem,
        scratch_shapes=[
            pltpu.VMEM((2 * first_rows, 2 * second_rows), jnp.bfloat16),
            pltpu.VMEM((2 * max(first_rows, second_rows), 2 * max(first_rows, second_rows)), jnp.float32),
            pltpu.VMEM((2 * first_rows, 2 * second_rows), jnp.bfloat16),
            pltpu.VMEM((first_rows // BLK, second_rows + 2 * PAD, BLK), jnp.float32),
            pltpu.VMEM((KCOH, count, rows, first_rows), jnp.float32),
            pltpu.VMEM((KCOH, count, rows, first_rows), jnp.float32),
            pltpu.SemaphoreType.DMA((KCOH,)),
            pltpu.SemaphoreType.DMA((KCOH,)),
        ],
        compiler_params=pltpu.CompilerParams(
            collective_id=0, has_side_effects=True, vmem_limit_bytes=60 << 20
        ),
    )(
        drift,
        strain_series.reshape(2, first_rows, second_rows),
        antenna.reshape(2, first_rows, second_rows),
        jnp.asarray(chirp_table(points, first_rows)),
        jnp.asarray(twist_table(points, first_rows)),
        jnp.asarray(dft_table(first_rows)),
        jnp.asarray(dft_table(second_rows)),
        jnp.concatenate([pick, pick], 1),
    )
    return summed / segments


def solution(mesh):
    return jax.shard_map(
        functools.partial(local, mesh.shape["seg"]),
        mesh=mesh,
        in_specs=(
            P(("sky", "seg"), None, None),
            P(("sky", "seg"), None, None),
            P(("sky", "seg"), None),
            P(),
        ),
        out_specs=P("sky", "seg"),
        check_vma=False,
    )
```

time: 318 us -> 58.3 us (0.18)
  waiting for transfers between devices: 180 us -> 0 us
  other arithmetic: 85.7 us -> 2.98 us
  Pallas kernels: 0 us -> 50.6 us
  matrix products: 18.4 us -> 0 us
  between operations: 16.9 us -> 0.02 us
  local copies, waits for them, and re-layouts: 16.4 us -> 4.42 us
    reduce_scatter x1 -> x0, waiting for transfers between devices: 180 us -> none  [local(): lax.psum_scatter(partial_sum, 'seg', scatter_dimension=1, tiled=True)]
    another operation x7 -> x0, other arithmetic: 65.7 us -> none
    pallas_call x0 -> x1, Pallas kernels: none -> 50.6 us  [local(): pl.pallas_call(functools.partial(kernel, count), out_shape=jax.ShapeDtype...]
    dot_general x3 -> x0, matrix products: 18.4 us -> none  [the longest x1 10.2 us: track_combine(): jnp.einsum('jsk,skf->jf', pick, moved, precision=lax.Precision.HIGHEST)]
    reshape x1 -> x0, local copies, waits for them, and re-layouts: 10.9 us -> none  [coherent_stat(): spectra = spectra.reshape(seg_rows, KCOH, 2, 2, points)]
    div x2 -> x1, other arithmetic: 12.2 us -> 2.27 us  [local(): return summed / segments]
    convert_element_type x1 -> x0, local copies, waits for them, and re-layouts: 5.43 us -> none  [coherent_stat(): weighted = jnp.stack([with_a, with_b], 2).astype(jnp.bfloat16)]
    unnamed x12 -> x2, local copies, waits for them, and re-layouts: 0.03 us -> 3.57 us
  transfers between devices with their start and end apart: 1 -> 0, of which waited for: 1 -> 0; matrix products, arithmetic and copies ran while one was open for 0% -> 0% of each run, Pallas kernels for 0% -> 0%
where the time goes in v1:
time: 58.3 us; the launch traced here: 58.1 us
  Pallas kernels  50.6 us (87%)
  local copies, waits for them, and re-layouts  4.42 us (8%)
  other arithmetic  2.98 us (5%)
    pallas_call x1, Pallas kernels, local(): pl.pallas_call(functools.partial(kernel, count), out_shape=jax.ShapeDtype...  50.6 us
    unnamed x2, local copies, waits for them, and re-layouts  3.57 us
    div x1, other arithmetic, local(): return summed / segments  2.27 us

profile of v1, /device:TPU:0, one launch (start us, length us, event | category | flops | bytes accessed | tf_op | source)
XLA Modules:
  0.0 58.1 jit_solution(2319469808305580348)
XLA Ops:
  0.0 0.1 eq.23
  0.1 0.7 %eq.20 = s32[64,6,16]{0,2,1:T(8,128)S(1)} broadcast(s32[64,16]{0,1:T(8,128)} %param.11), dimensions={0,2} | broadcast | bytes 28672 | tf_op jit(solution)/shard_map/eq | solution.py:169
  0.8 0.1 copy.10
  0.9 0.7 %add_convert_fusion.pick_ref = bf16[64,192]{1,0:T(8,128)(2,1)} fusion(pred[64,96]{1,0:T(8,128)(4,1)S(1)} %broadcast_compare_fusion), kind=kLoop, calls=%fused_computation.3 | loop fusion | flops 24576 | bytes 30720 | tf_op jit(solution)/shard_map/concatenate | solution.py:198
  1.6 1.7 %copy.16 = bf16[1,2,256,256]{3,2,1,0:T(8,128)(2,1)} copy(bf16[1,2,256,256]{3,1,2,0:T(2,128)(2,1)} %bitcast.14) | data formatting | bytes 524288
  3.3 1.9 %copy.15 = f32[1,2,256,256]{3,2,1,0:T(8,128)} copy(f32[1,2,256,256]{3,1,2,0:T(2,128)} %bitcast.13) | data formatting | bytes 1048576
  5.1 50.6 %shard_map.82 = f32[64,4096]{1,0:T(8,128)} custom-call(s32[1,6]{1,0:T(1,128)} %drift_ref.1, bf16[2,256,256]{2,1,0:T(8,128)(2,1)} %bitcast.12, f32[2,256,256]{2,1,0:T(8,128)} %bitcast.11, f32[3,2,256,256]{3,2,1,0:T(8,128)} %constant.9.clone.chirp_ref, f32[2,256,256]{2,1,0:T(8,128)} %constant.10.clone.twist_ref, ...), custom_call_target="tpu_custom_call" | custom-call | tf_op jit(solution)/shard_map/pallas_call | solution.py:172
  55.8 2.3 %broadcast_multiply_fusion = f32[64,4096]{1,0:T(8,128)} fusion(f32[64,4096]{1,0:T(8,128)} %shard_map.82), kind=kLoop, calls=%fused_computation.1 | loop fusion | flops 262144 | bytes 2097152 | tf_op jit(solution)/shard_map/div | solution.py:200
  (2 shorter events, 0.0 us)

commit v2 on v1

--- a/solution.py
+++ b/solution.py
@@ -43,10 +43,10 @@
 
 
 def kernel(
-    count, drift_ref, series_ref, antenna_ref, chirp_ref, twist_ref, first_ref, second_ref, pick_ref, out_ref,
-    weighted, spread, middle, padded, send, recv, send_sem, recv_sem,
+    count, drift_ref, series_ref, antenna_ref, chirp_ref, twist_ref, first_ref, second_ref, tracks_ref, out_ref,
+    strain, weights, weighted, spread, middle, padded, send, recv, send_sem, recv_sem,
 ):
-    _, first_rows, second_rows = series_ref.shape
+    _, first_rows, second_rows = strain.shape
     rows = second_rows // count
     points = first_rows * second_rows
     halves = first_rows // BLK
@@ -63,7 +63,15 @@
 
     lax.fori_loop(1, count, greet, 0)
 
-    weight_a, weight_b = antenna_ref[0], antenna_ref[1]
+    pieces = second_rows // BLK
+    for which in range(2):
+        for piece in range(pieces):
+            lanes = slice(piece * BLK, (piece + 1) * BLK)
+            lines = pl.ds(piece, first_rows, stride=pieces)
+            strain[which, :, lanes] = series_ref[lines, which, :]
+            weights[which, :, lanes] = antenna_ref[lines, which, :]
+
+    weight_a, weight_b = weights[0], weights[1]
     total = lambda value: jnp.sum(jnp.sum(value, axis=0, keepdims=True), axis=1, keepdims=True)
     aa = total(weight_a * weight_a) / points + tiny_eps
     bb = total(weight_b * weight_b) / points + tiny_eps
@@ -83,11 +91,11 @@
         sign = jnp.where(upper, 1.0, -1.0)
         chirp_cos = chirp_ref[level, 0]
         chirp_sin = chirp_ref[level, 1] * sign
-        real, imag = series_ref[0].astype(jnp.float32), series_ref[1].astype(jnp.float32)
+        real, imag = strain[0], strain[1]
         demod_real = real * chirp_cos + imag * chirp_sin
         demod_imag = imag * chirp_cos - real * chirp_sin
         for which in range(2):
-            weight = antenna_ref[which]
+            weight = weights[which]
             columns = slice(which * second_rows, (which + 1) * second_rows)
             weighted[:first_rows, columns] = (weight * demod_real).astype(jnp.bfloat16)
             weighted[first_rows:, columns] = (weight * demod_imag).astype(jnp.bfloat16)
@@ -143,17 +151,22 @@
 
     lax.fori_loop(0, KCOH, one_rate, 0)
 
-    for k in range(KCOH):
+    out_ref[...] = jnp.zeros_like(out_ref)
+
+    def collect(k, carry):
         pltpu.make_async_copy(recv.at[k], recv.at[k], recv_sem.at[k]).wait()
-
-    pick = pick_ref[...]
-    for row in range(rows):
-        value = recv[:, :, row, :].reshape(KCOH * count, first_rows)
-        high = value.astype(jnp.bfloat16)
-        low = (value - high.astype(jnp.float32)).astype(jnp.bfloat16)
-        out_ref[:, row * first_rows : (row + 1) * first_rows] = jnp.dot(
-            pick, jnp.concatenate([high, low], 0), preferred_element_type=jnp.float32
-        )
+        pick = jnp.where(tracks_ref[...] == k, 1.0, 0.0).astype(jnp.bfloat16)
+        for row in range(rows):
+            value = recv[k, :, row, :]
+            high = value.astype(jnp.bfloat16)
+            low = (value - high.astype(jnp.float32)).astype(jnp.bfloat16)
+            columns = slice(row * first_rows, (row + 1) * first_rows)
+            out_ref[:, columns] += jnp.dot(pick, high, preferred_element_type=jnp.float32) + jnp.dot(
+                pick, low, preferred_element_type=jnp.float32
+            )
+        return carry
+
+    lax.fori_loop(0, KCOH, collect, 0)
 
     for k in range(KCOH):
         part = send.at[k, pl.ds(0, count - 1)]
@@ -165,9 +178,7 @@
     first_rows, second_rows = DFT_ROWS, points // DFT_ROWS
     segments = tracks.shape[1]
     rows = second_rows // count
-    levels = jnp.arange(KCOH, dtype=jnp.int32)
-    pick = (tracks[:, None, :] == levels[None, :, None]).astype(jnp.bfloat16)
-    pick = pick.reshape(tracks.shape[0], KCOH * segments)
+    blocked = lambda array: array.reshape(2, points // BLK, BLK).transpose(1, 0, 2)
     vmem = pl.BlockSpec(memory_space=pltpu.VMEM)
     summed = pl.pallas_call(
         functools.partial(kernel, count),
@@ -175,6 +186,8 @@
         in_specs=[pl.BlockSpec(memory_space=pltpu.SMEM)] + [vmem] * 7,
         out_specs=vmem,
         scratch_shapes=[
+            pltpu.VMEM((2, first_rows, second_rows), jnp.float32),
+            pltpu.VMEM((2, first_rows, second_rows), jnp.float32),
             pltpu.VMEM((2 * first_rows, 2 * second_rows), jnp.bfloat16),
             pltpu.VMEM((2 * max(first_rows, second_rows), 2 * max(first_rows, second_rows)), jnp.float32),
             pltpu.VMEM((2 * first_rows, 2 * second_rows), jnp.bfloat16),
@@ -189,13 +202,13 @@
         ),
     )(
         drift,
-        strain_series.reshape(2, first_rows, second_rows),
-        antenna.reshape(2, first_rows, second_rows),
+        blocked(strain_series.astype(jnp.float32)),
+        blocked(antenna),
         jnp.asarray(chirp_table(points, first_rows)),
         jnp.asarray(twist_table(points, first_rows)),
         jnp.asarray(dft_table(first_rows)),
         jnp.asarray(dft_table(second_rows)),
-        jnp.concatenate([pick, pick], 1),
+        tracks,
     )
     return summed / segments
 

time: 58.3 us -> 52.6 us (0.902)
  Pallas kernels: 50.6 us -> 46.8 us
  local copies, waits for them, and re-layouts: 4.42 us -> 1.38 us
  other arithmetic: 2.98 us -> 4.19 us
    pallas_call x1, Pallas kernels: 50.6 us -> 46.8 us  [local(): pl.pallas_call(functools.partial(kernel, count), out_shape=jax.ShapeDtype...]
    unnamed x2 -> x1, local copies, waits for them, and re-layouts: 3.57 us -> 1.38 us
    transpose x0 -> x1, other arithmetic: none -> 1.92 us  [local(): array.reshape(2, points // BLK, BLK).transpose(1, 0, 2)]
    eq x4 -> x0, local copies, waits for them, and re-layouts: 0.86 us -> none  [local(): pick = (tracks[:, None, :] == levels[None, :, None]).astype(jnp.bfloat16)]
    concatenate x1 -> x0, other arithmetic: 0.69 us -> none  [local(): jnp.concatenate([pick, pick], 1)]
where the time goes in v2:
time: 52.6 us; the launch traced here: 52.4 us
  Pallas kernels  46.8 us (89%)
  other arithmetic  4.19 us (8%)
  local copies, waits for them, and re-layouts  1.38 us (3%)
    pallas_call x1, Pallas kernels, local(): pl.pallas_call(functools.partial(kernel, count), out_shape=jax.ShapeDtype...  46.8 us
    div x1, other arithmetic, local(): return summed / segments  2.27 us
    transpose x1, other arithmetic, local(): array.reshape(2, points // BLK, BLK).transpose(1, 0, 2)  1.92 us
    unnamed x1, local copies, waits for them, and re-layouts  1.38 us

profile of v2, /device:TPU:0, one launch (start us, length us, event | category | flops | bytes accessed | tf_op | source)
XLA Modules:
  0.0 52.4 jit_solution(5861000099932154758)
XLA Ops:
  0.0 1.4 %copy.9.tracks_ref = s32[64,16]{1,0:T(8,128)} copy(s32[64,16]{0,1:T(8,128)} %param.11) | data formatting | bytes 8192 | tf_op args[3]
  1.4 1.9 %convert_bitcast_fusion.series_ref = f32[512,2,128]{2,1,0:T(2,128)} fusion(bf16[1,2,65536]{2,1,0:T(2,128)(2,1)} %param.8), kind=kLoop, calls=%fused_computation | loop fusion | flops 131072 | bytes 786432 | tf_op jit(solution)/shard_map/transpose | solution.py:181
  3.3 46.8 %shard_map.82 = f32[64,4096]{1,0:T(8,128)} custom-call(s32[1,6]{1,0:T(1,128)} %drift_ref.1, f32[512,2,128]{2,1,0:T(2,128)} %convert_bitcast_fusion.series_ref, f32[512,2,128]{2,1,0:T(2,128)} %bitcast.8, f32[3,2,256,256]{3,2,1,0:T(8,128)} %constant.9.clone.chirp_ref, f32[2,256,256]{2,1,0:T(8,128)} %constant.10.clone.twist_ref, ...), custom_call_target="tpu_custom_call" | custom-call | tf_op jit(solution)/shard_map/pallas_call | solution.py:183
  50.1 2.3 %broadcast_multiply_fusion = f32[64,4096]{1,0:T(8,128)} fusion(f32[64,4096]{1,0:T(8,128)} %shard_map.82), kind=kLoop, calls=%fused_computation.1 | loop fusion | flops 262144 | bytes 2097152 | tf_op jit(solution)/shard_map/div | solution.py:213

commit v3 on v2

--- a/solution.py
+++ b/solution.py
@@ -144,14 +144,16 @@
             ).start()
             return inner
 
-        lax.fori_loop(count // 2, count, ship, 0)
-        lax.fori_loop(1, count // 2, ship, 0)
+        lax.fori_loop(1, count, ship, 0)
         pltpu.make_async_copy(send.at[k, me], recv.at[k, me], recv_sem.at[k]).start()
         return carry
 
     lax.fori_loop(0, KCOH, one_rate, 0)
 
     out_ref[...] = jnp.zeros_like(out_ref)
+    add_rows = lambda pick, value: lax.dot_general(
+        pick, value, (((0,), (0,)), ((), ())), preferred_element_type=jnp.float32
+    )
 
     def collect(k, carry):
         pltpu.make_async_copy(recv.at[k], recv.at[k], recv_sem.at[k]).wait()
@@ -161,9 +163,7 @@
             high = value.astype(jnp.bfloat16)
             low = (value - high.astype(jnp.float32)).astype(jnp.bfloat16)
             columns = slice(row * first_rows, (row + 1) * first_rows)
-            out_ref[:, columns] += jnp.dot(pick, high, preferred_element_type=jnp.float32) + jnp.dot(
-                pick, low, preferred_element_type=jnp.float32
-            )
+            out_ref[:, columns] += add_rows(pick, high) + add_rows(pick, low)
         return carry
 
     lax.fori_loop(0, KCOH, collect, 0)
@@ -182,7 +182,7 @@
     vmem = pl.BlockSpec(memory_space=pltpu.VMEM)
     summed = pl.pallas_call(
         functools.partial(kernel, count),
-        out_shape=jax.ShapeDtypeStruct((tracks.shape[0], points // count), jnp.float32),
+        out_shape=pltpu.VMEM((tracks.shape[0], points // count), jnp.float32),
         in_specs=[pl.BlockSpec(memory_space=pltpu.SMEM)] + [vmem] * 7,
         out_specs=vmem,
         scratch_shapes=[
@@ -208,7 +208,7 @@
         jnp.asarray(twist_table(points, first_rows)),
         jnp.asarray(dft_table(first_rows)),
         jnp.asarray(dft_table(second_rows)),
-        tracks,
+        tracks.T,
     )
     return summed / segments
 

time: 52.6 us -> 46.9 us (0.89)
  Pallas kernels: 46.8 us -> 43.8 us
  local copies, waits for them, and re-layouts: 1.38 us -> 0 us
  other arithmetic: 4.19 us -> 2.98 us
    pallas_call x1, Pallas kernels: 46.8 us -> 43.8 us  [local(): pl.pallas_call(functools.partial(kernel, count), out_shape=pltpu.VMEM((tr...]
    unnamed x1 -> x0, local copies, waits for them, and re-layouts: 1.38 us -> none
    div x1, other arithmetic: 2.27 us -> 1.06 us  [local(): return summed / segments]
where the time goes in v3:
time: 46.9 us; the launch traced here: 46.7 us
  Pallas kernels  43.8 us (93%)
  other arithmetic  2.98 us (6%)
    pallas_call x1, Pallas kernels, local(): pl.pallas_call(functools.partial(kernel, count), out_shape=pltpu.VMEM((tr...  43.8 us
    transpose x1, other arithmetic, local(): array.reshape(2, points // BLK, BLK).transpose(1, 0, 2)  1.92 us
    div x1, other arithmetic, local(): return summed / segments  1.06 us

profile of v3, /device:TPU:0, one launch (start us, length us, event | category | flops | bytes accessed | tf_op | source)
XLA Modules:
  0.0 46.7 jit_solution(6155728938581517257)
XLA Ops:
  0.0 1.9 %convert_bitcast_fusion.series_ref = f32[512,2,128]{2,1,0:T(2,128)} fusion(bf16[1,2,65536]{2,1,0:T(2,128)(2,1)} %param.8), kind=kLoop, calls=%fused_computation | loop fusion | flops 131072 | bytes 786432 | tf_op jit(solution)/shard_map/transpose | solution.py:181
  1.9 43.8 %shard_map.82 = f32[64,4096]{1,0:T(8,128)S(1)} custom-call(s32[1,6]{1,0:T(1,128)} %drift_ref.1, f32[512,2,128]{2,1,0:T(2,128)} %convert_bitcast_fusion.series_ref, f32[512,2,128]{2,1,0:T(2,128)} %bitcast.9, f32[3,2,256,256]{3,2,1,0:T(8,128)} %constant.9.clone.chirp_ref, f32[2,256,256]{2,1,0:T(8,128)} %constant.10.clone.twist_ref, ...), custom_call_target="tpu_custom_call" | custom-call | tf_op jit(solution)/shard_map/pallas_call | solution.py:183
  45.7 1.1 %broadcast_multiply_fusion = f32[64,4096]{1,0:T(8,128)} fusion(f32[64,4096]{1,0:T(8,128)S(1)} %shard_map.82), kind=kLoop, calls=%fused_computation.1 | loop fusion | flops 262144 | bytes 2097152 | tf_op jit(solution)/shard_map/div | solution.py:213
